TPU v7x, 32 devices: a whole 2x2x4 slice. The times are simulated.
32 devices in a mesh: groups: 2 (over x), expert: 16 (over z, y, core).
Axes of the slice: x: 2, y: 2, z: 4, core: 2. Of those that a mesh axis runs over, the one named last changes fastest.
Arguments:
- tokens: bfloat16 [2048, 2048], P(('groups', 'expert')), parts along dimension 0, may hold values from -6 to 6
- expert_ids: int32 [2048, 8], P(('groups', 'expert')), parts along dimension 0, may hold values from 0 to 15, as said below
- gate_weights: float32 [2048, 8], P(('groups', 'expert')), parts along dimension 0, may hold values from 0.05 to 0.5
- w_gate: bfloat16 [16, 2048, 768], P('expert'), may hold values from -0.125 to 0.125
- w_up: bfloat16 [16, 2048, 768], P('expert'), may hold values from -0.125 to 0.125
- w_down: bfloat16 [16, 768, 2048], P('expert'), may hold values from -0.21875 to 0.21875
Outputs:
- mixed: bfloat16 [2048, 2048], P(('groups', 'expert')), parts along dimension 0
There are 2 independent parts, one for each index of `groups`. A program takes and returns all parts, laid end to end along the dimension named above; an argument that names none is the same for every part. Nothing has to cross between parts.
Inputs may be any that keep to these rules, and one draw needn't show every extreme that they name: `expert_ids`: each token names 8 different experts. Exactly 2 experts are named exactly 64 times by the tokens of every device; every other expert is named at most 28 times by the tokens of one device, and in every draw some such expert is named exactly 28 times by the tokens of every device.
All inputs are finite; a program needn't handle non-finite values.
Results may differ from a plain program's by a relative error of at most 0.0057.
Values may be sent and summed in bfloat16 or wider, within the bound.
A program may use at most 128 MiB of HBM per device.

v0:
```python
import jax
import jax.numpy as jnp
from jax import lax
from jax.sharding import PartitionSpec as P

row_block = 256


def swiglu_rows(rows_in, weights):
    gate_part = jnp.dot(rows_in, weights[0], preferred_element_type=jnp.float32)
    up_part = jnp.dot(rows_in, weights[1], preferred_element_type=jnp.float32)
    hidden = (jax.nn.silu(gate_part) * up_part).astype(jnp.bfloat16)
    return jnp.dot(hidden, weights[2], preferred_element_type=jnp.float32).astype(jnp.bfloat16)


def run_blocks(source_rows, block_total, weights, results):

    def block_step(block_num, current):
        row_start = block_num * row_block
        rows_in = lax.dynamic_slice_in_dim(source_rows, row_start, row_block, 0)
        return lax.dynamic_update_slice_in_dim(current, swiglu_rows(rows_in, weights), row_start, 0)

    return lax.fori_loop(jnp.zeros((), jnp.int32), block_total, block_step, results)


def route_and_run(tokens, flat_ids, slot_rank, routed, capacity, device_count, own_weights):
    local_tokens, model_width = tokens.shape
    slot_total = flat_ids.shape[0]
    top_count = slot_total // local_tokens
    buffer_rows = device_count * capacity
    padded_rows = (buffer_rows + row_block - 1) // row_block * row_block
    send_slot = jnp.where(routed, flat_ids * capacity + slot_rank, buffer_rows)
    token_of_slot = jnp.arange(slot_total, dtype=jnp.int32) // top_count
    source_row = jnp.zeros((buffer_rows,), jnp.int32).at[send_slot].set(token_of_slot, mode="drop")
    slot_filled = jnp.zeros((buffer_rows,), jnp.int32).at[send_slot].set(1, mode="drop")
    send_counts = jnp.sum(slot_filled.reshape(device_count, capacity), axis=1)
    outgoing = jnp.where(slot_filled[:, None] > 0, tokens[source_row], jnp.zeros((), jnp.bfloat16))
    outgoing = outgoing.reshape(device_count, capacity, model_width)
    count_column = send_counts.astype(jnp.bfloat16).reshape(device_count, 1)
    incoming, arrived = (
        lax.all_to_all(outgoing, "expert", split_axis=0, concat_axis=0, tiled=True),
        lax.all_to_all(count_column, "expert", split_axis=0, concat_axis=0, tiled=True),
    )
    arrived_counts = arrived.reshape(-1).astype(jnp.int32)
    offsets = jnp.cumsum(arrived_counts) - arrived_counts
    live_total = jnp.sum(arrived_counts)
    slot_index = jnp.arange(buffer_rows, dtype=jnp.int32)
    source_of = slot_index // capacity
    within = slot_index % capacity
    is_live = within < arrived_counts[source_of]
    packed_pos = offsets[source_of] + within
    target_pos = jnp.where(is_live, packed_pos, padded_rows)
    compact_source = (
        jnp.full((padded_rows,), buffer_rows, jnp.int32).at[target_pos].set(slot_index, mode="drop")
    )
    flat_incoming = jnp.concatenate(
        [incoming.reshape(buffer_rows, model_width), jnp.zeros((1, model_width), jnp.bfloat16)],
        axis=0,
    )
    compact = flat_incoming[compact_source]
    block_need = (live_total + row_block - 1) // row_block
    results = run_blocks(
        compact, block_need, own_weights, jnp.zeros((padded_rows, model_width), jnp.bfloat16)
    )
    back_slots = results[jnp.where(is_live, packed_pos, 0)]
    back_slots = jnp.where(is_live[:, None], back_slots, jnp.zeros((), jnp.bfloat16))
    back_slots = back_slots.reshape(device_count, capacity, model_width)
    returned_rows = lax.all_to_all(back_slots, "expert", split_axis=0, concat_axis=0, tiled=True)
    picked = returned_rows.reshape(buffer_rows, model_width)[jnp.where(routed, send_slot, 0)]
    return jnp.where(routed[:, None], picked, jnp.zeros((), jnp.bfloat16))


def shards(tokens, expert_ids, gate_weights, w_gate, w_up, w_down):
    device_count = lax.axis_size("expert")
    local_tokens, model_width = tokens.shape
    top_count = expert_ids.shape[1]
    expert_total = device_count * w_gate.shape[0]
    capacity = min(
        local_tokens, 4 * ((local_tokens * top_count + expert_total - 1) // expert_total)
    )
    flat_ids = expert_ids.reshape(-1)
    slot_total = flat_ids.shape[0]
    expert_range = jnp.arange(device_count, dtype=jnp.int32)
    onehot = (flat_ids[:, None] == expert_range[None, :]).astype(jnp.int32)
    slot_rank = jnp.sum(jnp.cumsum(onehot, axis=0) * onehot, axis=1) - 1
    own_weights = (w_gate[0], w_up[0], w_down[0])
    routed = jnp.ones((slot_total,), jnp.bool_)
    slot_values = route_and_run(
        tokens, flat_ids, slot_rank, routed, capacity, device_count, own_weights
    )
    picked = slot_values.reshape(local_tokens, top_count, model_width)
    mixed = jnp.sum(picked.astype(jnp.float32) * gate_weights[:, :, None], axis=1)
    return mixed.astype(jnp.bfloat16)


def solution(mesh):
    placed = (
        P(("groups", "expert"), None),
        P(("groups", "expert"), None),
        P(("groups", "expert"), None),
        P("expert", None, None),
        P("expert", None, None),
        P("expert", None, None),
    )
    return jax.shard_map(
        shards, mesh=mesh, in_specs=placed, out_specs=P(("groups", "expert"), None), check_vma=False
    )
```

profile of v0, /device:TPU:15, one launch (start us, length us, event | category | flops | bytes accessed | tf_op | source)
XLA Modules:
  0.0 305.7 jit_solution(18314291863465316378)
XLA Ops:
  0.0 0.0 copy-start
  0.0 0.8 copy.30
  0.8 0.1 eq.31
  0.9 0.1 eq.27
  1.0 0.7 broadcast_multiply_fusion
  1.7 1.1 reduce-window.19
  2.8 0.2 slice_reduce_fusion
  3.1 0.1 fusion.14
  3.2 0.1 copy.29
  3.3 0.1 mul.40
  3.4 2.4 scatter_custom_fusion
  5.9 0.1 reshape.244
  5.9 0.1 reduce_sum.37
  6.1 0.7 copy.33
  6.8 6.5 %all-to-all-start = ((bf16[16,1,1]{2,1,0:T(2,128)(2,1)}), bf16[16,1,1]{2,1,0:T(2,128)(2,1)S(1)}, u32[]{:S(2)}, u32[]{:S(2)}) async-start(bf16[16,1,1]{2,1,0:T(2,128)(2,1)} %copy.33), calls=%async_computation | async-start | bytes 16384 | tf_op jit(solution)/shard_map/all_to_all | solution.py:42
  13.3 0.1 broadcast_in_dim.61
  13.4 2.4 scatter_custom_fusion.1
  15.9 6.0 %gather_fusion = bf16[1024,2048]{1,0:T(8,128)(2,1)} fusion(bf16[64,2048]{1,0:T(8,128)(2,1)S(1)} %copy-done, s32[1024]{0:T(1024)S(1)} %fusion.20), kind=kCustom, calls=%fused_computation | custom fusion | bytes 8392704 | tf_op jit(solution)/shard_map/gather | solution.py:37
  21.9 4.5 %broadcast_select_fusion = bf16[16,64,2048]{2,1,0:T(8,128)(2,1)} fusion(bf16[16,64,2048]{2,1,0:T(8,128)(2,1)} %bitcast.78, pred[16,64]{1,0:T(8,128)(4,1)S(1)} %broadcast_in_dim.61), kind=kLoop, calls=%fused_computation.20 | loop fusion | flops 2097152 | bytes 8389632 | tf_op jit(solution)/shard_map/jit(_where)/select_n | solution.py:37
  26.4 0.0 all-to-all-done
  26.4 6.0 %all-to-all-start.1 = ((bf16[16,64,2048]{2,1,0:T(8,128)(2,1)}), bf16[16,64,2048]{2,1,0:T(8,128)(2,1)}, u32[]{:S(2)}, u32[]{:S(2)}) async-start(bf16[16,64,2048]{2,1,0:T(8,128)(2,1)} %broadcast_select_fusion), calls=%async_computation.1 | async-start | bytes 8388608 | tf_op jit(solution)/shard_map/all_to_all | solution.py:41
  32.7 0.9 convert_reduce_fusion.1
  34.3 0.1 reduce.11
  34.4 0.6 fusion.33
  35.1 4.2 %compare_select_fusion.6 = s32[1024,1]{0,1:T(1,128)S(1)} fusion(s32[]{:T(128)} %bitcast.13, s32[]{:T(128)} %bitcast.14, s32[]{:T(128)} %bitcast.15, s32[]{:T(128)} %bitcast.16, s32[]{:T(128)} %bitcast.17, s32[]{:T(128)} %bitcast.19, s32[]{:T(128)} %bitcast.18), kind=kLoop, calls=%fused_computation.48 | loop fusion | flops 23552 | bytes 4124 | tf_op jit(solution)/shard_map/gather | solution.py:50
  39.3 5.7 %select_select_fusion.1 = s32[1024]{0:T(1024)S(1)} fusion(pred[1024]{0:T(1024)(128)(4,1)S(1)} %compare_reduce_fusion, pred[1024]{0:T(1024)(128)(4,1)S(1)} %compare_reduce_fusion.1, pred[1024]{0:T(1024)(128)(4,1)S(1)} %compare_reduce_fusion.2, pred[1024]{0:T(1024)(128)(4,1)S(1)} %compare_reduce_fusion.3, pred[1024]{0:T(1024)(128)(4,1)S(1)} %compare_reduce_fusion.4, ...), kind=kLoop, calls=%fused_computation.72 | loop fusion | flops 9216 | bytes 17444 | tf_op jit(solution)/shard_map/gather | solution.py:50
  45.0 0.1 gather.29
  45.1 0.7 fusion.34
  45.8 4.5 %compare_select_fusion.7 = s32[1024,1]{0,1:T(1,128)S(1)} fusion(s32[]{:T(128)} %bitcast.34, s32[]{:T(128)} %bitcast.35, s32[]{:T(128)} %bitcast.36, s32[]{:T(128)} %bitcast.37, s32[]{:T(128)} %bitcast.38, s32[]{:T(128)} %bitcast.40, s32[]{:T(128)} %bitcast.39), kind=kLoop, calls=%fused_computation.49 | loop fusion | flops 23552 | bytes 4124 | tf_op jit(solution)/shard_map/gather | solution.py:51
  50.3 5.4 %select_select_fusion = s32[1024]{0:T(1024)S(1)} fusion(pred[1024]{0:T(1024)(128)(4,1)S(1)} %compare_reduce_fusion, pred[1024]{0:T(1024)(128)(4,1)S(1)} %compare_reduce_fusion.1, pred[1024]{0:T(1024)(128)(4,1)S(1)} %compare_reduce_fusion.2, pred[1024]{0:T(1024)(128)(4,1)S(1)} %compare_reduce_fusion.3, pred[1024]{0:T(1024)(128)(4,1)S(1)} %compare_reduce_fusion.4, ...), kind=kLoop, calls=%fused_computation.71 | loop fusion | flops 9216 | bytes 17444 | tf_op jit(solution)/shard_map/gather | solution.py:51
  55.8 4.3 %scatter_custom_fusion.2 = s32[1024]{0:T(1024)S(1)} fusion(s32[1024]{0:T(1024)S(1)} %bitcast.89, s32[1024]{0:T(1024)S(1)} %iota.46, s32[]{:T(128)} %constant.94.clone.1), kind=kCustom, calls=%fused_computation.80 | custom fusion | bytes 4100 | tf_op jit(solution)/shard_map/scatter | solution.py:54
  60.2 64.7 %all-to-all-done.1 = bf16[16,64,2048]{2,1,0:T(8,128)(2,1)} async-done(((bf16[16,64,2048]{2,1,0:T(8,128)(2,1)}), bf16[16,64,2048]{2,1,0:T(8,128)(2,1)}, u32[]{:S(2)}, u32[]{:S(2)}) %all-to-all-start.1) | async-done | bytes 4194336 | tf_op jit(solution)/shard_map/all_to_all | solution.py:41
  124.8 4.7 %concatenate.3 = bf16[1025,2048]{1,0:T(8,128)(2,1)} pad(bf16[1024,2048]{1,0:T(8,128)(2,1)} %bitcast.22, bf16[]{:T(256)} %constant.98.clone.1), padding=0_1x0_0 | pad | bytes 8392706 | tf_op jit(solution)/shard_map/concatenate | solution.py:56
  129.6 11.6 %gather_fusion.1 = bf16[1024,2048]{1,0:T(8,128)(2,1)} fusion(bf16[1025,2048]{1,0:T(8,128)(2,1)} %concatenate.3, s32[1024]{0:T(1024)S(1)} %fusion.21), kind=kCustom, calls=%fused_computation.1 | custom fusion | bytes 8392704 | tf_op jit(solution)/shard_map/gather | solution.py:60
  141.1 2.5 broadcast_in_dim.60
  143.6 0.4 copy-done.2
  144.0 19.3 %while.10 = (s32[]{:T(128)}, bf16[1024,2048]{1,0:T(8,128)(2,1)}, s32[]{:T(128)}, bf16[1024,2048]{1,0:T(8,128)(2,1)}, bf16[2048,768]{1,0:T(8,128)(2,1)S(1)}, /*in...) while((s32[]{:T(128)}, bf16[1024,2048]{1,0:T(8,128)(2,1)}, ...), condition=%wide.region_10.11_spmd, body=%wide.region_9.10_spmd.sunk | while | flops 2417623040 | bytes 14156959 | solution.py:23
  144.0 3.1 %fusion.50 = f32[256,768]{1,0:T(8,128)} fusion(bf16[2048,768]{1,0:T(8,128)(2,1)S(1)} %get-tuple-element.164, bf16[1024,2048]{1,0:T(8,128)(2,1)} %get-tuple-element.163, s32[]{:T(128)S(6)} %select_n.234), kind=kOutput, calls=%fused_computation.12.clone.1 | convolution fusion | flops 805306368 | bytes 4980740 | tf_op jit(solution)/shard_map/while/body/dot_general | solution.py:10
  147.2 6.6 %fusion.51 = bf16[1024,2048]{1,0:T(8,128)(2,1)} fusion(bf16[1024,2048]{1,0:T(8,128)(2,1)} %get-tuple-element.150, s32[]{:T(128)S(6)} %select_n.234, bf16[768,2048]{1,0:T(8,128)(2,1)} %get-tuple-element.166, bf16[2048,768]{1,0:T(8,128)(2,1)} %get-tuple-element.165, bf16[1024,2048]{1,0:T(8,128)(2,1)} %get-tuple-element.163, f32[256,768]{1,0:T(8,128)} %fusion.50), kind=kOutput, calls=%fused_computation.8.clone.1 | convolution fusion | flops 1612316672 | bytes 9176064 | tf_op jit(solution)/shard_map/while/body/dot_general | solution.py:13
  153.7 3.1 %fusion.50 = f32[256,768]{1,0:T(8,128)} fusion(bf16[2048,768]{1,0:T(8,128)(2,1)S(1)} %get-tuple-element.164, bf16[1024,2048]{1,0:T(8,128)(2,1)} %get-tuple-element.163, s32[]{:T(128)S(6)} %select_n.234), kind=kOutput, calls=%fused_computation.12.clone.1 | convolution fusion | flops 805306368 | bytes 4980740 | tf_op jit(solution)/shard_map/while/body/dot_general | solution.py:10
  156.8 6.5 %fusion.51 = bf16[1024,2048]{1,0:T(8,128)(2,1)} fusion(bf16[1024,2048]{1,0:T(8,128)(2,1)} %get-tuple-element.150, s32[]{:T(128)S(6)} %select_n.234, bf16[768,2048]{1,0:T(8,128)(2,1)} %get-tuple-element.166, bf16[2048,768]{1,0:T(8,128)(2,1)} %get-tuple-element.165, bf16[1024,2048]{1,0:T(8,128)(2,1)} %get-tuple-element.163, f32[256,768]{1,0:T(8,128)} %fusion.50), kind=kOutput, calls=%fused_computation.8.clone.1 | convolution fusion | flops 1612316672 | bytes 9176064 | tf_op jit(solution)/shard_map/while/body/dot_general | solution.py:13
  163.3 11.6 %gather_fusion.2 = bf16[1024,2048]{1,0:T(8,128)(2,1)} fusion(bf16[1024,2048]{1,0:T(8,128)(2,1)} %get-tuple-element.43, s32[1024]{0:T(1024)S(1)} %broadcast_clamp_fusion), kind=kCustom, calls=%fused_computation.2 | custom fusion | bytes 8392704 | tf_op jit(solution)/shard_map/gather | solution.py:65
  174.9 4.5 %broadcast_select_fusion.1 = bf16[16,64,2048]{2,1,0:T(8,128)(2,1)} fusion(bf16[16,64,2048]{2,1,0:T(8,128)(2,1)} %bitcast.77, pred[16,64]{1,0:T(8,128)(4,1)S(1)} %fusion.16), kind=kLoop, calls=%fused_computation.21 | loop fusion | flops 2097152 | bytes 8389632 | tf_op jit(solution)/shard_map/jit(_where)/select_n | solution.py:66
  179.4 24.2 %all-to-all-start.2 = ((bf16[16,64,2048]{2,1,0:T(8,128)(2,1)}), bf16[16,64,2048]{2,1,0:T(8,128)(2,1)}, u32[]{:S(2)}, u32[]{:S(2)}) async-start(bf16[16,64,2048]{2,1,0:T(8,128)(2,1)} %broadcast_select_fusion.1), calls=%async_computation.2 | async-start | bytes 8388608 | tf_op jit(solution)/shard_map/all_to_all | solution.py:68
  203.6 0.1 copy.35
  203.7 92.4 %all-to-all-done.2 = bf16[16,64,2048]{2,1,0:T(8,128)(2,1)} async-done(((bf16[16,64,2048]{2,1,0:T(8,128)(2,1)}), bf16[16,64,2048]{2,1,0:T(8,128)(2,1)}, u32[]{:S(2)}, u32[]{:S(2)}) %all-to-all-start.2) | async-done | bytes 4194336 | tf_op jit(solution)/shard_map/all_to_all | solution.py:68
  296.0 7.1 %gather_fusion.3 = bf16[512,2048]{1,0:T(8,128)(2,1)S(1)} fusion(bf16[1024,2048]{1,0:T(8,128)(2,1)} %bitcast.49, s32[1024]{0:T(1024)S(1)} %pad_clamp_fusion), kind=kCustom, calls=%fused_computation.3 | custom fusion | bytes 4196352 | tf_op jit(solution)/shard_map/gather | solution.py:69
  303.2 2.5 fusion.12
  (32 shorter events, 0.5 us)
Async XLA Ops:
  0.0 15.9 %copy-start = (bf16[64,2048]{1,0:T(8,128)(2,1)S(1)}, bf16[64,2048]{1,0:T(8,128)(2,1)}, u32[]{:S(2)}) copy-start(bf16[64,2048]{1,0:T(8,128)(2,1)} %param.8) | copy-start | bytes 786436
  6.8 19.6 %all-to-all-start = ((bf16[16,1,1]{2,1,0:T(2,128)(2,1)}), bf16[16,1,1]{2,1,0:T(2,128)(2,1)S(1)}, u32[]{:S(2)}, u32[]{:S(2)}) async-start(bf16[16,1,1]{2,1,0:T(2,128)(2,1)} %copy.33), calls=%async_computation | async-start | bytes 16384 | tf_op jit(solution)/shard_map/all_to_all | solution.py:42
  26.4 98.5 %all-to-all-start.1 = ((bf16[16,64,2048]{2,1,0:T(8,128)(2,1)}), bf16[16,64,2048]{2,1,0:T(8,128)(2,1)}, u32[]{:S(2)}, u32[]{:S(2)}) async-start(bf16[16,64,2048]{2,1,0:T(8,128)(2,1)} %broadcast_select_fusion), calls=%async_computation.1 | async-start | bytes 8388608 | tf_op jit(solution)/shard_map/all_to_all | solution.py:41
  141.1 2.9 copy-start.2
  179.4 24.2 %copy-start.1 = (f32[64,8]{0,1:T(8,128)S(1)}, f32[64,8]{0,1:T(8,128)}, u32[]{:S(2)}) copy-start(f32[64,8]{0,1:T(8,128)} %param.10) | copy-start | bytes 6148
  179.4 116.6 %all-to-all-start.2 = ((bf16[16,64,2048]{2,1,0:T(8,128)(2,1)}), bf16[16,64,2048]{2,1,0:T(8,128)(2,1)}, u32[]{:S(2)}, u32[]{:S(2)}) async-start(bf16[16,64,2048]{2,1,0:T(8,128)(2,1)} %broadcast_select_fusion.1), calls=%async_computation.2 | async-start | bytes 8388608 | tf_op jit(solution)/shard_map/all_to_all | solution.py:68
where the time goes:
time: 307 us; the launch traced here: 306 us
  waiting for transfers between devices  157 us (51%)
  local copies, waits for them, and re-layouts  56.8 us (19%)
  starting transfers between devices  36.7 us (12%)
  other arithmetic  35 us (11%)
  matrix products  19.3 us (6%)
    all_to_all x1, waiting for transfers between devices, route_and_run(): lax.all_to_all(back_slots, 'expert', split_axis=0, concat_axis=0, tiled=T...  92.4 us
    all_to_all x1, waiting for transfers between devices, route_and_run(): lax.all_to_all(outgoing, 'expert', split_axis=0, concat_axis=0, tiled=True)  64.7 us
    all_to_all x1, starting transfers between devices, route_and_run(): lax.all_to_all(back_slots, 'expert', split_axis=0, concat_axis=0, tiled=T...  24.2 us
    dot_general x2, matrix products, swiglu_rows(): jnp.dot(hidden, weights[2], preferred_element_type=jnp.float32)  13.1 us
    gather x1, local copies, waits for them, and re-layouts, route_and_run(): compact = flat_incoming[compact_source]  11.6 us
    gather x1, local copies, waits for them, and re-layouts, route_and_run(): back_slots = results[jnp.where(is_live, packed_pos, 0)]  11.6 us
    gather x11, other arithmetic, route_and_run(): is_live = within < arrived_counts[source_of]  10.2 us
    gather x2, other arithmetic, route_and_run(): packed_pos = offsets[source_of] + within  9.94 us
  transfers between devices with their start and end apart: 3, of which 2 were waited for; matrix products, arithmetic and copies ran while one was open for 13% of the time, Pallas kernels for 0%

commit v1 on v0

--- a/solution.py
+++ b/solution.py
@@ -4,6 +4,39 @@
 from jax.sharding import PartitionSpec as P
 
 row_block = 256
+
+
+def measure_desk_in(my_data, axis_k, shard_in):
+    latest = my_data.shape
+    tile_out = my_data.reshape(
+        *latest[:axis_k], shard_in, latest[axis_k] // shard_in, *latest[axis_k + 1 :]
+    )
+    return jnp.moveaxis(tile_out, axis_k, 0)
+
+
+def pairs_all_show(mat, where_dim):
+    block_last = list(mat.shape[1:])
+    block_last[where_dim] *= mat.shape[0]
+    return jnp.moveaxis(mat, 0, where_dim).reshape(block_last)
+
+
+def values_time(chunk, axis_key, original, w_in):
+    x_new = lax.axis_size(axis_key)
+    after = lax.axis_index(axis_key)
+    row_out, reply = (x_new, after)
+    k_now = measure_desk_in(chunk, original, row_out)
+    pile = [k_now[reply]]
+    for w in range(1, row_out):
+        long_array = k_now[(reply + w) % row_out]
+        m_next = lax.ppermute(
+            long_array,
+            axis_name=axis_key,
+            perm=[(dev_j, (dev_j + w) % row_out) for dev_j in range(row_out)],
+        )
+        pile.append(m_next)
+    arr_out = jnp.stack(pile, axis=0)
+    k_now = arr_out[(reply - jnp.arange(row_out)) % row_out]
+    return pairs_all_show(k_now, w_in)
 
 
 def swiglu_rows(rows_in, weights):
@@ -38,7 +71,7 @@
     outgoing = outgoing.reshape(device_count, capacity, model_width)
     count_column = send_counts.astype(jnp.bfloat16).reshape(device_count, 1)
     incoming, arrived = (
-        lax.all_to_all(outgoing, "expert", split_axis=0, concat_axis=0, tiled=True),
+        values_time(outgoing, "expert", 0, 0),
         lax.all_to_all(count_column, "expert", split_axis=0, concat_axis=0, tiled=True),
     )
     arrived_counts = arrived.reshape(-1).astype(jnp.int32)

time: 307 us -> 342 us (1.11)
  local copies, waits for them, and re-layouts: 56.8 us -> 78.7 us
  waiting for transfers between devices: 157 us -> 168 us
  starting transfers between devices: 36.7 us -> 40.9 us
    all_to_all x1 -> x0, waiting for transfers between devices: 64.7 us -> none  [route_and_run(): lax.all_to_all(outgoing, 'expert', split_axis=0, concat_axis=0, tiled=True)]
    ppermute x0 -> x15, waiting for transfers between devices: none -> 56.6 us  [values_time(): lax.ppermute(long_array, axis_name=axis_key, perm=[(dev_j, (dev_j + w) %...]
    all_to_all x1, waiting for transfers between devices: 0.01 us -> 19 us  [route_and_run(): lax.all_to_all(count_column, 'expert', split_axis=0, concat_axis=0, tiled...]
    ppermute x0 -> x15, starting transfers between devices: none -> 17.2 us  [values_time(): lax.ppermute(long_array, axis_name=axis_key, perm=[(dev_j, (dev_j + w) %...]
    unnamed x8 -> x22, local copies, waits for them, and re-layouts: 1.31 us -> 16.3 us
    all_to_all x1 -> x0, starting transfers between devices: 6.02 us -> none  [route_and_run(): lax.all_to_all(outgoing, 'expert', split_axis=0, concat_axis=0, tiled=True)]
    all_to_all x1, starting transfers between devices: 24.2 us -> 18.6 us  [route_and_run(): lax.all_to_all(back_slots, 'expert', split_axis=0, concat_axis=0, tiled=T...]
    gather x0 -> x1, local copies, waits for them, and re-layouts: none -> 4.96 us  [values_time(): k_now = arr_out[(reply - jnp.arange(row_out)) % row_out]]
  transfers between devices with their start and end apart: 3 -> 17, of which waited for: 2 -> 7; matrix products, arithmetic and copies ran while one was open for 13% -> 13% of each run, Pallas kernels for 0% -> 0%
where the time goes in v1:
time: 342 us; the launch traced here: 341 us
  waiting for transfers between devices  168 us (49%)
  local copies, waits for them, and re-layouts  78.7 us (23%)
  starting transfers between devices  40.9 us (12%)
  other arithmetic  32.9 us (10%)
  matrix products  19.3 us (6%)
    all_to_all x1, waiting for transfers between devices, route_and_run(): lax.all_to_all(back_slots, 'expert', split_axis=0, concat_axis=0, tiled=T...  92.4 us
    ppermute x15, waiting for transfers between devices, values_time(): lax.ppermute(long_array, axis_name=axis_key, perm=[(dev_j, (dev_j + w) %...  56.6 us
    all_to_all x1, waiting for transfers between devices, route_and_run(): lax.all_to_all(count_column, 'expert', split_axis=0, concat_axis=0, tiled...  19 us
    all_to_all x1, starting transfers between devices, route_and_run(): lax.all_to_all(back_slots, 'expert', split_axis=0, concat_axis=0, tiled=T...  18.6 us
    ppermute x15, starting transfers between devices, values_time(): lax.ppermute(long_array, axis_name=axis_key, perm=[(dev_j, (dev_j + w) %...  17.2 us
    unnamed x22, local copies, waits for them, and re-layouts  16.3 us
    gather x7, other arithmetic, route_and_run(): is_live = within < arrived_counts[source_of]  14.4 us
    dot_general x2, matrix products, swiglu_rows(): jnp.dot(hidden, weights[2], preferred_element_type=jnp.float32)  13.1 us
  transfers between devices with their start and end apart: 17, of which 7 were waited for; matrix products, arithmetic and copies ran while one was open for 13% of the time, Pallas kernels for 0%

profile of v1, /device:TPU:15, one launch (start us, length us, event | category | flops | bytes accessed | tf_op | source)
XLA Modules:
  0.0 340.7 jit_solution(8039249460953919788)
XLA Ops:
  0.0 0.8 copy.30
  1.7 1.2 reduce-window.19
  3.4 2.4 scatter_custom_fusion
  6.0 2.4 scatter_custom_fusion.1
  8.5 6.0 %gather_fusion = bf16[1024,2048]{1,0:T(8,128)(2,1)} fusion(bf16[64,2048]{1,0:T(8,128)(2,1)S(1)} %copy-done, s32[1024]{0:T(1024)S(1)} %fusion.20), kind=kCustom, calls=%fused_computation | custom fusion | bytes 8392704 | tf_op jit(solution)/shard_map/gather | solution.py:70
  14.6 2.5 broadcast_select_fusion
  17.1 1.3 dynamic-slice_bitcast_fusion
  18.4 1.8 collective-permute-start
  20.2 1.2 collective-permute-start.1
  21.7 1.0 collective-permute-start.3
  22.7 2.7 collective-permute-start.4
  26.3 5.1 %all-to-all-start = ((bf16[16,1,1]{2,1,0:T(2,128)(2,1)}), bf16[16,1,1]{2,1,0:T(2,128)(2,1)S(1)}, u32[]{:S(2)}, u32[]{:S(2)}) async-start(bf16[16,1,1]{2,1,0:T(2,128)(2,1)} %copy.33), calls=%async_computation | async-start | bytes 16384 | tf_op jit(solution)/shard_map/all_to_all | solution.py:75
  31.5 19.0 %all-to-all-done = bf16[16,1,1]{2,1,0:T(2,128)(2,1)S(1)} async-done(((bf16[16,1,1]{2,1,0:T(2,128)(2,1)}), bf16[16,1,1]{2,1,0:T(2,128)(2,1)S(1)}, u32[]{:S(2)}, u32[]{:S(2)}) %all-to-all-start) | async-done | bytes 64 | tf_op jit(solution)/shard_map/all_to_all | solution.py:75
  51.3 0.9 convert_reduce_fusion.1
  53.0 8.7 %compare_select_fusion.6 = (s32[1024,1]{0,1:T(1,128)S(1)}, s32[1024,1]{0,1:T(1,128)S(1)}) fusion(s32[]{:T(128)} %bitcast.13, s32[]{:T(128)} %bitcast.14, s32[]{:T(128)} %bitcast.15, s32[]{:T(128)} %bitcast.16, s32[]{:T(128)} %bitcast.17, s32[]{:T(128)} %bitcast.19, s32[]{:T(128)} %bitcast.18, s32[]{:T(128)} %bitcast.72, s32[]{:T(128)} %bitcast.71, ...), kind=kLoop, calls=%fused_computation.80 | loop fusion | flops 29696 | bytes 8248 | tf_op jit(solution)/shard_map/gather | solution.py:83
  61.7 5.6 %select_select_fusion = s32[1024]{0:T(1024)S(1)} fusion(pred[1024]{0:T(1024)(128)(4,1)S(1)} %get-tuple-element.110, pred[1024]{0:T(1024)(128)(4,1)S(1)} %get-tuple-element.111, pred[1024]{0:T(1024)(128)(4,1)S(1)} %get-tuple-element.112, pred[1024]{0:T(1024)(128)(4,1)S(1)} %get-tuple-element.113, pred[1024]{0:T(1024)(128)(4,1)S(1)} %get-tuple-element.114, ...), kind=kLoop, calls=%fused_computation.104 | loop fusion | flops 9216 | bytes 17444 | tf_op jit(solution)/shard_map/gather | solution.py:84
  67.3 5.6 %select_select_fusion.1 = s32[1024]{0:T(1024)S(1)} fusion(pred[1024]{0:T(1024)(128)(4,1)S(1)} %get-tuple-element.110, pred[1024]{0:T(1024)(128)(4,1)S(1)} %get-tuple-element.111, pred[1024]{0:T(1024)(128)(4,1)S(1)} %get-tuple-element.112, pred[1024]{0:T(1024)(128)(4,1)S(1)} %get-tuple-element.113, pred[1024]{0:T(1024)(128)(4,1)S(1)} %get-tuple-element.114, ...), kind=kLoop, calls=%fused_computation.105 | loop fusion | flops 9216 | bytes 17444 | tf_op jit(solution)/shard_map/gather | solution.py:83
  72.9 4.3 %scatter_custom_fusion.2 = s32[1024]{0:T(1024)S(1)} fusion(s32[1024]{0:T(1024)S(1)} %bitcast.154, s32[1024]{0:T(1024)S(1)} %iota.51, s32[]{:T(128)} %constant.186.clone.1), kind=kCustom, calls=%fused_computation.116 | custom fusion | bytes 4100 | tf_op jit(solution)/shard_map/scatter | solution.py:87
  78.0 2.7 collective-permute-start.5
  80.7 1.7 bitcast_dynamic-update-slice_fusion.14
  82.4 1.4 collective-permute-start.6
  83.9 1.7 bitcast_dynamic-update-slice_fusion.13
  85.5 1.5 collective-permute-start.7
  87.0 1.7 bitcast_dynamic-update-slice_fusion.12
  89.3 1.7 bitcast_dynamic-update-slice_fusion.11
  90.9 1.4 collective-permute-start.9
  92.4 1.7 bitcast_dynamic-update-slice_fusion.10
  94.0 26.1 %collective-permute-done.5 = bf16[1,64,2048]{2,1,0:T(8,128)(2,1)S(1)} collective-permute-done((bf16[1,64,2048]{2,1,0:T(8,128)(2,1)S(1)}, bf16[1,64,2048]{2,1,0:T(8,128)(2,1)S(1)}, u32[]{:S(2)}, u32[]{:S(2)}) %collective-permute-start.5) | collective-permute-done | bytes 262176 | tf_op jit(solution)/shard_map/ppermute | solution.py:31
  120.9 4.9 %collective-permute-done.6 = bf16[1,64,2048]{2,1,0:T(8,128)(2,1)S(1)} collective-permute-done((bf16[1,64,2048]{2,1,0:T(8,128)(2,1)S(1)}, bf16[1,64,2048]{2,1,0:T(8,128)(2,1)S(1)}, u32[]{:S(2)}, u32[]{:S(2)}) %collective-permute-start.6) | collective-permute-done | bytes 262176 | tf_op jit(solution)/shard_map/ppermute | solution.py:31
  126.5 10.5 %collective-permute-done.7 = bf16[1,64,2048]{2,1,0:T(8,128)(2,1)S(1)} collective-permute-done((bf16[1,64,2048]{2,1,0:T(8,128)(2,1)S(1)}, bf16[1,64,2048]{2,1,0:T(8,128)(2,1)S(1)}, u32[]{:S(2)}, u32[]{:S(2)}) %collective-permute-start.7) | collective-permute-done | bytes 262176 | tf_op jit(solution)/shard_map/ppermute | solution.py:31
  138.5 2.5 collective-permute-start.14
  143.2 0.9 collective-permute-done.12
  144.8 14.2 %collective-permute-done.13 = bf16[1,64,2048]{2,1,0:T(8,128)(2,1)S(1)} collective-permute-done((bf16[1,64,2048]{2,1,0:T(8,128)(2,1)S(1)}, bf16[1,64,2048]{2,1,0:T(8,128)(2,1)S(1)}, u32[]{:S(2)}, u32[]{:S(2)}) %collective-permute-start.13) | collective-permute-done | bytes 262176 | tf_op jit(solution)/shard_map/ppermute | solution.py:31
  160.4 5.0 %gather_fusion.1 = bf16[16,64,2048]{2,1,0:T(8,128)(2,1)} fusion(bf16[16,64,2048]{2,1,0:T(8,128)(2,1)} %bitcast.143, s32[1024]{0:T(1024)S(1)} %pad_clamp_fusion.1), kind=kCustom, calls=%fused_computation.1 | custom fusion | bytes 8388672 | tf_op jit(solution)/shard_map/gather | solution.py:38
  165.4 4.7 %concatenate.3 = bf16[1025,2048]{1,0:T(8,128)(2,1)} pad(bf16[1024,2048]{1,0:T(8,128)(2,1)} %bitcast.142, bf16[]{:T(256)} %constant.190.clone.1), padding=0_1x0_0 | pad | bytes 8392706 | tf_op jit(solution)/shard_map/concatenate | solution.py:89
  170.1 11.6 %gather_fusion.2 = bf16[1024,2048]{1,0:T(8,128)(2,1)} fusion(bf16[1025,2048]{1,0:T(8,128)(2,1)} %concatenate.3, s32[1024]{0:T(1024)S(1)} %fusion.21), kind=kCustom, calls=%fused_computation.2 | custom fusion | bytes 8392704 | tf_op jit(solution)/shard_map/gather | solution.py:93
  181.7 2.4 broadcast_in_dim.63
  184.6 19.3 %while.10 = (s32[]{:T(128)}, bf16[1024,2048]{1,0:T(8,128)(2,1)}, s32[]{:T(128)}, bf16[1024,2048]{1,0:T(8,128)(2,1)}, bf16[2048,768]{1,0:T(8,128)(2,1)S(1)}, /*in...) while((s32[]{:T(128)}, bf16[1024,2048]{1,0:T(8,128)(2,1)}, ...), condition=%wide.region_10.11_spmd, body=%wide.region_9.10_spmd.sunk | while | flops 2417623040 | bytes 14156959 | solution.py:56
  184.6 3.1 fusion.52
  187.7 6.5 %fusion.53 = bf16[1024,2048]{1,0:T(8,128)(2,1)} fusion(bf16[1024,2048]{1,0:T(8,128)(2,1)} %get-tuple-element.176, s32[]{:T(128)S(6)} %select_n.414, bf16[768,2048]{1,0:T(8,128)(2,1)} %get-tuple-element.192, bf16[2048,768]{1,0:T(8,128)(2,1)} %get-tuple-element.191, bf16[1024,2048]{1,0:T(8,128)(2,1)} %get-tuple-element.189, f32[256,768]{1,0:T(8,128)} %fusion.52), kind=kOutput, calls=%fused_computation.9.clone.1 | convolution fusion | flops 1612316672 | bytes 9176064 | tf_op jit(solution)/shard_map/while/body/dot_general | solution.py:46
  194.2 3.1 fusion.52
  197.4 6.6 %fusion.53 = bf16[1024,2048]{1,0:T(8,128)(2,1)} fusion(bf16[1024,2048]{1,0:T(8,128)(2,1)} %get-tuple-element.176, s32[]{:T(128)S(6)} %select_n.414, bf16[768,2048]{1,0:T(8,128)(2,1)} %get-tuple-element.192, bf16[2048,768]{1,0:T(8,128)(2,1)} %get-tuple-element.191, bf16[1024,2048]{1,0:T(8,128)(2,1)} %get-tuple-element.189, f32[256,768]{1,0:T(8,128)} %fusion.52), kind=kOutput, calls=%fused_computation.9.clone.1 | convolution fusion | flops 1612316672 | bytes 9176064 | tf_op jit(solution)/shard_map/while/body/dot_general | solution.py:46
  203.9 11.6 %gather_fusion.3 = bf16[1024,2048]{1,0:T(8,128)(2,1)} fusion(bf16[1024,2048]{1,0:T(8,128)(2,1)} %get-tuple-element.43, s32[1024]{0:T(1024)S(1)} %broadcast_clamp_fusion), kind=kCustom, calls=%fused_computation.3 | custom fusion | bytes 8392704 | tf_op jit(solution)/shard_map/gather | solution.py:98
  215.5 4.5 %broadcast_select_fusion.1 = bf16[16,64,2048]{2,1,0:T(8,128)(2,1)} fusion(bf16[16,64,2048]{2,1,0:T(8,128)(2,1)} %bitcast.140, pred[16,64]{1,0:T(8,128)(4,1)S(1)} %fusion.16), kind=kLoop, calls=%fused_computation.22 | loop fusion | flops 2097152 | bytes 8389632 | tf_op jit(solution)/shard_map/jit(_where)/select_n | solution.py:99
  219.9 18.6 %all-to-all-start.1 = ((bf16[16,64,2048]{2,1,0:T(8,128)(2,1)}), bf16[16,64,2048]{2,1,0:T(8,128)(2,1)}, u32[]{:S(2)}, u32[]{:S(2)}) async-start(bf16[16,64,2048]{2,1,0:T(8,128)(2,1)} %broadcast_select_fusion.1), calls=%async_computation.1 | async-start | bytes 8388608 | tf_op jit(solution)/shard_map/all_to_all | solution.py:101
  238.7 92.4 %all-to-all-done.1 = bf16[16,64,2048]{2,1,0:T(8,128)(2,1)} async-done(((bf16[16,64,2048]{2,1,0:T(8,128)(2,1)}), bf16[16,64,2048]{2,1,0:T(8,128)(2,1)}, u32[]{:S(2)}, u32[]{:S(2)}) %all-to-all-start.1) | async-done | bytes 4194336 | tf_op jit(solution)/shard_map/all_to_all | solution.py:101
  331.0 7.1 %gather_fusion.4 = bf16[512,2048]{1,0:T(8,128)(2,1)S(1)} fusion(bf16[1024,2048]{1,0:T(8,128)(2,1)} %bitcast.81, s32[1024]{0:T(1024)S(1)} %pad_clamp_fusion), kind=kCustom, calls=%fused_computation.4 | custom fusion | bytes 4196352 | tf_op jit(solution)/shard_map/gather | solution.py:102
  338.2 2.5 fusion.12
  (74 shorter events, 13.0 us)
Async XLA Ops:
  0.0 8.5 %copy-start = (bf16[64,2048]{1,0:T(8,128)(2,1)S(1)}, bf16[64,2048]{1,0:T(8,128)(2,1)}, u32[]{:S(2)}) copy-start(bf16[64,2048]{1,0:T(8,128)(2,1)} %param.8) | copy-start | bytes 786436
  18.4 59.6 %collective-permute-start = (bf16[1,64,2048]{2,1,0:T(8,128)(2,1)}, bf16[1,64,2048]{2,1,0:T(8,128)(2,1)}, u32[]{:S(2)}, u32[]{:S(2)}) collective-permute-start(bf16[1,64,2048]{2,1,0:T(8,128)(2,1)} %get-tuple-element.74), channel_id=1, source_target_pairs={{0,1},{1,2},{2,3},{3,4},{4,5},{5,6},{6,7},{7,8},{8,9},{9,10},{10,1... | collective-permute-start | bytes 786440 | tf_op jit(solution)/shard_map/ppermute | solution.py:31
  20.2 62.2 %collective-permute-start.1 = (bf16[1,64,2048]{2,1,0:T(8,128)(2,1)}, bf16[1,64,2048]{2,1,0:T(8,128)(2,1)}, u32[]{:S(2)}, u32[]{:S(2)}) collective-permute-start(bf16[1,64,2048]{2,1,0:T(8,128)(2,1)} %get-tuple-element.73), channel_id=1, source_target_pairs={{0,2},{1,3},{2,4},{3,5},{4,6},{5,7},{6,8},{7,9},{8,10},{9,11},{10,... | collective-permute-start | bytes 786440 | tf_op jit(solution)/shard_map/ppermute | solution.py:31
  21.4 64.1 %collective-permute-start.2 = (bf16[1,64,2048]{2,1,0:T(8,128)(2,1)}, bf16[1,64,2048]{2,1,0:T(8,128)(2,1)}, u32[]{:S(2)}, u32[]{:S(2)}) collective-permute-start(bf16[1,64,2048]{2,1,0:T(8,128)(2,1)} %get-tuple-element.72), channel_id=1, source_target_pairs={{0,3},{1,4},{2,5},{3,6},{4,7},{5,8},{6,9},{7,10},{8,11},{9,12},{10... | collective-permute-start | bytes 786440 | tf_op jit(solution)/shard_map/ppermute | solution.py:31
  21.7 66.9 %collective-permute-start.3 = (bf16[1,64,2048]{2,1,0:T(8,128)(2,1)S(1)}, bf16[1,64,2048]{2,1,0:T(8,128)(2,1)}, u32[]{:S(2)}, u32[]{:S(2)}) collective-permute-start(bf16[1,64,2048]{2,1,0:T(8,128)(2,1)S(1)} %get-tuple-element.71), channel_id=1, source_target_pairs={{0,4},{1,5},{2,6},{3,7},{4,8},{5,9},{6,10},{7,11},{8,12},{9,13},{1... | collective-permute-start | bytes 786440 | tf_op jit(solution)/shard_map/ppermute | solution.py:31
  22.7 68.2 %collective-permute-start.4 = (bf16[1,64,2048]{2,1,0:T(8,128)(2,1)S(1)}, bf16[1,64,2048]{2,1,0:T(8,128)(2,1)}, u32[]{:S(2)}, u32[]{:S(2)}) collective-permute-start(bf16[1,64,2048]{2,1,0:T(8,128)(2,1)S(1)} %get-tuple-element.70), channel_id=1, source_target_pairs={{0,5},{1,6},{2,7},{3,8},{4,9},{5,10},{6,11},{7,12},{8,13},{9,14},{... | collective-permute-start | bytes 786440 | tf_op jit(solution)/shard_map/ppermute | solution.py:31
  26.3 24.2 %all-to-all-start = ((bf16[16,1,1]{2,1,0:T(2,128)(2,1)}), bf16[16,1,1]{2,1,0:T(2,128)(2,1)S(1)}, u32[]{:S(2)}, u32[]{:S(2)}) async-start(bf16[16,1,1]{2,1,0:T(2,128)(2,1)} %copy.33), calls=%async_computation | async-start | bytes 16384 | tf_op jit(solution)/shard_map/all_to_all | solution.py:75
  78.0 42.1 %collective-permute-start.5 = (bf16[1,64,2048]{2,1,0:T(8,128)(2,1)S(1)}, bf16[1,64,2048]{2,1,0:T(8,128)(2,1)S(1)}, u32[]{:S(2)}, u32[]{:S(2)}) collective-permute-start(bf16[1,64,2048]{2,1,0:T(8,128)(2,1)S(1)} %get-tuple-element.69), channel_id=1, source_target_pairs={{0,6},{1,7},{2,8},{3,9},{4,10},{5,11},{6,12},{7,13},{8,14},{9,15},... | collective-permute-start | bytes 786440 | tf_op jit(solution)/shard_map/ppermute | solution.py:31
  82.4 43.3 %collective-permute-start.6 = (bf16[1,64,2048]{2,1,0:T(8,128)(2,1)S(1)}, bf16[1,64,2048]{2,1,0:T(8,128)(2,1)S(1)}, u32[]{:S(2)}, u32[]{:S(2)}) collective-permute-start(bf16[1,64,2048]{2,1,0:T(8,128)(2,1)S(1)} %get-tuple-element.68), channel_id=1, source_target_pairs={{0,7},{1,8},{2,9},{3,10},{4,11},{5,12},{6,13},{7,14},{8,15},{9,0},... | collective-permute-start | bytes 786440 | tf_op jit(solution)/shard_map/ppermute | solution.py:31
  85.5 51.5 %collective-permute-start.7 = (bf16[1,64,2048]{2,1,0:T(8,128)(2,1)S(1)}, bf16[1,64,2048]{2,1,0:T(8,128)(2,1)S(1)}, u32[]{:S(2)}, u32[]{:S(2)}) collective-permute-start(bf16[1,64,2048]{2,1,0:T(8,128)(2,1)S(1)} %get-tuple-element.67), channel_id=1, source_target_pairs={{0,8},{1,9},{2,10},{3,11},{4,12},{5,13},{6,14},{7,15},{8,0},{9,1},... | collective-permute-start | bytes 786440 | tf_op jit(solution)/shard_map/ppermute | solution.py:31
  88.7 49.0 %collective-permute-start.8 = (bf16[1,64,2048]{2,1,0:T(8,128)(2,1)S(1)}, bf16[1,64,2048]{2,1,0:T(8,128)(2,1)S(1)}, u32[]{:S(2)}, u32[]{:S(2)}) collective-permute-start(bf16[1,64,2048]{2,1,0:T(8,128)(2,1)S(1)} %get-tuple-element.66), channel_id=1, source_target_pairs={{0,9},{1,10},{2,11},{3,12},{4,13},{5,14},{6,15},{7,0},{8,1},{9,2},... | collective-permute-start | bytes 786440 | tf_op jit(solution)/shard_map/ppermute | solution.py:31
  90.9 47.5 %collective-permute-start.9 = (bf16[1,64,2048]{2,1,0:T(8,128)(2,1)S(1)}, bf16[1,64,2048]{2,1,0:T(8,128)(2,1)S(1)}, u32[]{:S(2)}, u32[]{:S(2)}) collective-permute-start(bf16[1,64,2048]{2,1,0:T(8,128)(2,1)S(1)} %get-tuple-element.65), channel_id=1, source_target_pairs={{0,10},{1,11},{2,12},{3,13},{4,14},{5,15},{6,0},{7,1},{8,2},{9,3},... | collective-permute-start | bytes 786440 | tf_op jit(solution)/shard_map/ppermute | solution.py:31
  120.1 21.6 %collective-permute-start.10 = (bf16[1,64,2048]{2,1,0:T(8,128)(2,1)S(1)}, bf16[1,64,2048]{2,1,0:T(8,128)(2,1)S(1)}, u32[]{:S(2)}, u32[]{:S(2)}) collective-permute-start(bf16[1,64,2048]{2,1,0:T(8,128)(2,1)S(1)} %get-tuple-element.64), channel_id=1, source_target_pairs={{0,11},{1,12},{2,13},{3,14},{4,15},{5,0},{6,1},{7,2},{8,3},{9,4},{... | collective-permute-start | bytes 786440 | tf_op jit(solution)/shard_map/ppermute | solution.py:31
  125.8 16.7 %collective-permute-start.11 = (bf16[1,64,2048]{2,1,0:T(8,128)(2,1)S(1)}, bf16[1,64,2048]{2,1,0:T(8,128)(2,1)S(1)}, u32[]{:S(2)}, u32[]{:S(2)}) collective-permute-start(bf16[1,64,2048]{2,1,0:T(8,128)(2,1)S(1)} %get-tuple-element.63), channel_id=1, source_target_pairs={{0,12},{1,13},{2,14},{3,15},{4,0},{5,1},{6,2},{7,3},{8,4},{9,5},{1... | collective-permute-start | bytes 786440 | tf_op jit(solution)/shard_map/ppermute | solution.py:31
  137.0 7.1 %collective-permute-start.12 = (bf16[1,64,2048]{2,1,0:T(8,128)(2,1)S(1)}, bf16[1,64,2048]{2,1,0:T(8,128)(2,1)S(1)}, u32[]{:S(2)}, u32[]{:S(2)}) collective-permute-start(bf16[1,64,2048]{2,1,0:T(8,128)(2,1)S(1)} %get-tuple-element.62), channel_id=1, source_target_pairs={{0,13},{1,14},{2,15},{3,0},{4,1},{5,2},{6,3},{7,4},{8,5},{9,6},{10... | collective-permute-start | bytes 786440 | tf_op jit(solution)/shard_map/ppermute | solution.py:31
  137.7 21.2 %collective-permute-start.13 = (bf16[1,64,2048]{2,1,0:T(8,128)(2,1)S(1)}, bf16[1,64,2048]{2,1,0:T(8,128)(2,1)S(1)}, u32[]{:S(2)}, u32[]{:S(2)}) collective-permute-start(bf16[1,64,2048]{2,1,0:T(8,128)(2,1)S(1)} %get-tuple-element.61), channel_id=1, source_target_pairs={{0,14},{1,15},{2,0},{3,1},{4,2},{5,3},{6,4},{7,5},{8,6},{9,7},{10,... | collective-permute-start | bytes 786440 | tf_op jit(solution)/shard_map/ppermute | solution.py:31
  138.5 21.2 %collective-permute-start.14 = (bf16[1,64,2048]{2,1,0:T(8,128)(2,1)S(1)}, bf16[1,64,2048]{2,1,0:T(8,128)(2,1)S(1)}, u32[]{:S(2)}, u32[]{:S(2)}) collective-permute-start(bf16[1,64,2048]{2,1,0:T(8,128)(2,1)S(1)} %get-tuple-element.60), channel_id=1, source_target_pairs={{0,15},{1,0},{2,1},{3,2},{4,3},{5,4},{6,5},{7,6},{8,7},{9,8},{10,9... | collective-permute-start | bytes 786440 | tf_op jit(solution)/shard_map/ppermute | solution.py:31
  181.7 2.9 copy-start.2
  219.9 18.6 %copy-start.1 = (f32[64,8]{0,1:T(8,128)S(1)}, f32[64,8]{0,1:T(8,128)}, u32[]{:S(2)}) copy-start(f32[64,8]{0,1:T(8,128)} %param.10) | copy-start | bytes 6148
  219.9 111.1 %all-to-all-start.1 = ((bf16[16,64,2048]{2,1,0:T(8,128)(2,1)}), bf16[16,64,2048]{2,1,0:T(8,128)(2,1)}, u32[]{:S(2)}, u32[]{:S(2)}) async-start(bf16[16,64,2048]{2,1,0:T(8,128)(2,1)} %broadcast_select_fusion.1), calls=%async_computation.1 | async-start | bytes 8388608 | tf_op jit(solution)/shard_map/all_to_all | solution.py:101
